TPU v7x, 32 devices: a whole 2x2x4 slice. The times are simulated.
32 devices in a mesh: rows: 8 (over z, x), scales: 4 (over y, core).
Axes of the slice: x: 2, y: 2, z: 4, core: 2. Of those that a mesh axis runs over, the one named last changes fastest.
Arguments:
- image_now: float32 [256, 8192], P(('rows', 'scales')), may hold values from 0.1 to 4
- gradient: float32 [256, 8192], P(('rows', 'scales')), may hold values from -140 to 140
- hessian_weight: float32 [256, 8192], P(('rows', 'scales')), may hold values from 0.1 to 10
- psf_tiles: float32 [32, 256], P(('rows', 'scales')), may hold values from -0.5 to 1.7
- facet_of_row: int32 [256], P(('rows', 'scales')), may hold values from 0 to 31, never falling along the last dimension, each value on 1 to 32 neighbouring positions
- tile_slot: int32 [32], replicated, may hold values from 0 to 31, each once
- thresholds: float32 [4], replicated, may hold values from 0.2 to 2
Outputs:
- new_image: float32 [256, 8192], P(('rows', 'scales'))
Inputs may be any that keep to these rules, and one draw needn't show every extreme that they name: `facet_of_row`: facet numbers never fall along the rows; every facet covers 1 to 32 rows, and some facet exactly 32. `tile_slot`: each facet's tile stands in a different row of psf_tiles, and every row holds one.
All inputs are finite; a program needn't handle non-finite values.
Results may differ from a plain program's by a relative error of at most 0.0001.
Values sent between devices are 32-bit elements; how exact they have to be, the bound alone decides.
A program may use at most 64 MiB of HBM per device.

v0:
```python
import jax
import jax.numpy as jnp
from jax import lax
from jax.sharding import PartitionSpec as P

TILE = 16
SUBITERS = 2
SPLINE_EDGE = 0.0625
SPLINE_NEAR = 0.25
SPLINE_MID = 0.375


def padded_2(cells, sides, width):
    for axis, dim in sides:
        count = lax.axis_size(axis)
        ends = count - 1
        head = lax.slice_in_dim(cells, 0, width, axis=dim)
        tail = lax.slice_in_dim(cells, cells.shape[dim] - width, cells.shape[dim], axis=dim)
        cells = jnp.concatenate(
            [
                lax.ppermute(tail, axis, [(i, (i + 1) % count) for i in range(ends)]),
                cells,
                lax.ppermute(head, axis, [((i + 1) % count, i) for i in range(ends)]),
            ],
            axis=dim,
        )
    return cells


def along_columns(source, spacing):
    length = source.shape[1]
    padded = jnp.pad(source, ((0, 0), (2 * spacing, 2 * spacing)))
    outer_pair = padded[:, 0:length] + padded[:, 4 * spacing : 4 * spacing + length]
    inner_pair = (
        padded[:, spacing : spacing + length] + padded[:, 3 * spacing : 3 * spacing + length]
    )
    return SPLINE_EDGE * outer_pair + SPLINE_NEAR * inner_pair + SPLINE_MID * source


def rows_traced(source, spacing, reach):
    length = source.shape[0]
    padded = jnp.pad(source, ((reach, reach), (0, 0)))

    def shifted_rows(offset):
        return lax.dynamic_slice_in_dim(padded, reach + offset, length, 0)

    outer_pair = shifted_rows(-2 * spacing) + shifted_rows(2 * spacing)
    inner_pair = shifted_rows(-spacing) + shifted_rows(spacing)
    return SPLINE_EDGE * outer_pair + SPLINE_NEAR * inner_pair + SPLINE_MID * source


def widen_band(source):
    half_tile = TILE // 2
    extended = padded_2(source, ((("rows", "scales"), 0),), half_tile)
    return jnp.pad(extended, ((0, 0), (half_tile, half_tile)))


def forward_blur(source, weights):
    band_rows, columns = source.shape
    padded = widen_band(source)

    def forward_add_tap_row(tap_row, summed):
        shifted = lax.dynamic_slice_in_dim(padded, tap_row, band_rows, 0)
        tap_weights = lax.dynamic_index_in_dim(weights, tap_row, 1, keepdims=False)
        for column in range(TILE):
            summed = (
                summed + tap_weights[:, column : column + 1] * shifted[:, column : column + columns]
            )
        return summed

    return lax.fori_loop(0, TILE, forward_add_tap_row, jnp.zeros((band_rows, columns), jnp.float32))


def adjoint_blur(source, wide_weights):
    band_rows, columns = source.shape
    half_tile = TILE // 2
    padded = widen_band(source)

    def adjoint_add_tap_row(tap_row, summed):
        offset = 2 * half_tile - tap_row
        shifted = lax.dynamic_slice_in_dim(padded, offset, band_rows, 0)
        weight_rows = lax.dynamic_slice_in_dim(wide_weights, offset, band_rows, 0)
        tap_weights = lax.dynamic_index_in_dim(weight_rows, tap_row, 1, keepdims=False)
        for column in range(TILE):
            offset_col = 2 * half_tile - column
            summed = (
                summed
                + tap_weights[:, column : column + 1]
                * shifted[:, offset_col : offset_col + columns]
            )
        return summed

    return lax.fori_loop(0, TILE, adjoint_add_tap_row, jnp.zeros((band_rows, columns), jnp.float32))


def body(image_now, gradient, hessian_weight, psf_tiles, facet_of_row, tile_slot, thresholds):
    band_rows, columns = image_now.shape
    half_tile = TILE // 2
    scale_count = lax.axis_size("scales")
    scale_index = lax.axis_index("scales")
    facet_ids = jnp.arange(tile_slot.shape[0], dtype=jnp.int32)
    slot_rows = jnp.sum(
        jnp.where(facet_of_row[:, None] == facet_ids[None, :], tile_slot[None, :], 0), axis=1
    )
    tiles_in = lax.all_gather(psf_tiles, ("rows", "scales"), axis=0, tiled=True)
    length = tiles_in.shape[0]
    onehot = (slot_rows[:, None] == jnp.arange(length, dtype=jnp.int32)[None, :]).astype(
        jnp.float32
    )
    flat_rows = jnp.dot(
        onehot, tiles_in, precision=lax.Precision.HIGHEST, preferred_element_type=jnp.float32
    )
    wide_rows = padded_2(flat_rows, ((("rows", "scales"), 0),), half_tile)
    weights = flat_rows.reshape(band_rows, TILE, TILE)
    wide_weights = wide_rows.reshape(band_rows + 2 * half_tile, TILE, TILE)
    level_gain = jnp.sum(jnp.where(jnp.arange(scale_count) == scale_index, thresholds, 0.0))
    reach = 2**scale_count

    def column_level(depth, plane):
        return rows_traced(plane, jnp.left_shift(jnp.int32(1), depth), reach)

    current = image_now
    for sweep in range(SUBITERS):
        change = current - image_now
        pushed = hessian_weight * forward_blur(change, weights)
        descent = gradient + adjoint_blur(pushed, wide_weights)
        blurred = forward_blur(descent, weights)
        totals = lax.psum(
            (jnp.sum(descent * descent), jnp.sum(hessian_weight * blurred * blurred)),
            ("rows", "scales"),
        )
        step_size = totals[0] / totals[1]
        trial = current - step_size * descent
        stripe = lax.all_gather(trial, "scales", axis=0, tiled=True)
        smooth = stripe
        lower = jnp.zeros_like(stripe)
        upper = jnp.zeros_like(stripe)
        for depth in range(scale_count):
            smoother = along_columns(smooth, 2**depth)
            lower = jnp.where(scale_index == depth, smooth, lower)
            upper = jnp.where(scale_index == depth, smoother, upper)
            smooth = smoother
        limit = step_size * level_gain
        lower_cols, upper_cols = (
            lax.all_to_all(lower, "rows", split_axis=1, concat_axis=0, tiled=True),
            lax.all_to_all(upper, "rows", split_axis=1, concat_axis=0, tiled=True),
        )
        lower_cols = lax.fori_loop(0, scale_index, column_level, lower_cols)
        upper_cols = lax.fori_loop(0, scale_index + 1, column_level, upper_cols)
        detail = lower_cols - upper_cols
        kept = (
            detail
            - jnp.clip(detail, -limit, limit)
            + jnp.where(scale_index == scale_count - 1, upper_cols, 0.0)
        )
        contribution = lax.all_to_all(kept, "rows", split_axis=0, concat_axis=1, tiled=True)
        current = lax.psum_scatter(contribution, "scales", scatter_dimension=0, tiled=True)
    return current


def solution(mesh):
    in_specs = (
        P(("rows", "scales"), None),
        P(("rows", "scales"), None),
        P(("rows", "scales"), None),
        P(("rows", "scales"), None),
        P(("rows", "scales")),
        P(),
        P(),
    )
    out_specs = P(("rows", "scales"), None)
    return jax.shard_map(body, mesh=mesh, in_specs=in_specs, out_specs=out_specs, check_vma=False)
```

profile of v0, /device:TPU:0, one launch (start us, length us, event | category | flops | bytes accessed | tf_op | source)
XLA Modules:
  0.0 672.7 jit_solution(16924233468898300590)
XLA Ops:
  12.2 45.4 %all-gather = f32[32,1,256]{2,1,0:T(1,128)S(1)} all-gather(f32[1,1,256]{2,1,0:T(1,128)} %bitcast.79), channel_id=1, replica_groups=mesh['rows'=8,'scales'=4] {'rows','scales'}, dimensions={0}, use_global_device_ids=true | all-gather | bytes 33792 | tf_op jit(solution)/shard_map/all_gather | solution.py:105
  58.2 27.8 %while.146 = (s32[]{:T(128)}, f32[8,8192]{1,0:T(8,128)S(1)}, f32[8,16,16]{2,0,1:T(8,128)S(1)}, f32[24,8208]{1,0:T(8,128)S(1)}, s32[]{:T(128)}, /*index=5*/s32[]{...) while((s32[]{:T(128)}, f32[8,8192]{1,0:T(8,128)S(1)}, ...), condition=%wide.region_2.3_spmd.clone, body=%wide.region_1.2_spmd.clone.sunk | while | flops 2162706 | bytes 4721599 | solution.py:71
  97.0 29.6 %while.147 = (s32[]{:T(128)}, f32[8,8192]{1,0:T(8,128)S(1)}, f32[24,16,16]{2,0,1:T(8,128)S(1)}, f32[24,8208]{1,0:T(8,128)S(1)}, s32[]{:T(128)}, /*index=5*/s32[]...) while((s32[]{:T(128)}, f32[8,8192]{1,0:T(8,128)S(1)}, ...), condition=%wide.region_4.5_spmd.clone, body=%wide.region_3.4_spmd.clone.sunk | while | flops 2162713 | bytes 4721729 | solution.py:93
  127.3 4.3 collective-permute-start.6
  135.3 27.8 %while.148 = (s32[]{:T(128)}, f32[8,8192]{1,0:T(8,128)S(1)}, f32[8,16,16]{2,0,1:T(8,128)S(1)}, f32[24,8208]{1,0:T(8,128)S(1)}, s32[]{:T(128)}, /*index=5*/s32[]{...) while((s32[]{:T(128)}, f32[8,8192]{1,0:T(8,128)S(1)}, ...), condition=%wide.region_8.9_spmd.clone, body=%wide.region_7.8_spmd.clone.sunk | while | flops 2162706 | bytes 4721599 | solution.py:71
  163.9 42.4 %all-reduce.19 = (f32[]{:T(128)}, f32[]{:T(128)}) all-reduce(f32[]{:T(128)} %get-tuple-element.1221, f32[]{:T(128)} %fusion.137), channel_id=1, replica_groups=mesh['rows'=8,'scales'=4] {'rows','scales'}, use_global_device_ids=true, to_apply=%region_6.7 | all-reduce | flops 2 | bytes 16 | tf_op jit(solution)/shard_map/psum | solution.py:128
  208.5 17.4 %all-gather.4.cloned.1.call-done = f32[32,8192]{1,0:T(8,128)} async-done(((f32[8,8192]{1,0:T(8,128)}), f32[32,8192]{1,0:T(8,128)}) %all-gather.4.cloned.1.call-update) | async-done | bytes 1048592 | tf_op jit(solution)/shard_map/all_gather | solution.py:134
  236.8 5.5 all-to-all-start.1
  243.4 25.1 %all-to-all-done.1 = f32[32,8,1024]{2,0,1:T(8,128)S(1)} async-done(((f32[32,8,1024]{2,0,1:T(8,128)}), f32[32,8,1024]{2,0,1:T(8,128)S(1)}, u32[]{:S(2)}, u32[]{:S(2)}) %all-to-all-start.1) | async-done | bytes 1048608 | tf_op jit(solution)/shard_map/all_to_all | solution.py:146
  274.4 23.8 %all-to-all-done = f32[32,8,1024]{2,0,1:T(8,128)S(1)} async-done(((f32[32,8,1024]{2,0,1:T(8,128)}), f32[32,8,1024]{2,0,1:T(8,128)S(1)}, u32[]{:S(2)}, u32[]{:S(2)}) %all-to-all-start) | async-done | bytes 1048608 | tf_op jit(solution)/shard_map/all_to_all | solution.py:145
  298.5 30.1 %all_to_all.114 = f32[8,32,1024]{2,1,0:T(8,128)S(1)} all-to-all(f32[8,32,1024]{2,1,0:T(8,128)S(1)} %bitcast.72), channel_id=1, replica_groups=mesh['rows'=8,'scales'=4] {'rows'}, dimensions={0} | all-to-all | bytes 2097152 | tf_op jit(solution)/shard_map/all_to_all | solution.py:156
  329.9 24.7 %reduce-scatter.3.cloned.1.call-done = f32[8,8192]{1,0:T(8,128)} async-done(((f32[32,8192]{1,0:T(8,128)}), f32[8,8192]{1,0:T(8,128)}) %reduce-scatter.3.cloned.1.call-update) | async-done | bytes 262160 | tf_op jit(solution)/shard_map/reduce_scatter | solution.py:157
  361.2 27.8 %while.149 = (s32[]{:T(128)}, f32[8,8192]{1,0:T(8,128)S(1)}, f32[8,16,16]{2,0,1:T(8,128)S(1)}, f32[24,8208]{1,0:T(8,128)S(1)}, s32[]{:T(128)}, /*index=5*/s32[]{...) while((s32[]{:T(128)}, f32[8,8192]{1,0:T(8,128)S(1)}, ...), condition=%wide.region_18.19_spmd.clone, body=%wide.region_17.18_spmd.clone.sunk | while | flops 2162706 | bytes 4721599 | solution.py:71
  389.0 6.7 collective-permute-start.10
  399.4 29.6 %while.150 = (s32[]{:T(128)}, f32[8,8192]{1,0:T(8,128)S(1)}, f32[24,16,16]{2,0,1:T(8,128)S(1)}, f32[24,8208]{1,0:T(8,128)S(1)}, s32[]{:T(128)}, /*index=5*/s32[]...) while((s32[]{:T(128)}, f32[8,8192]{1,0:T(8,128)S(1)}, ...), condition=%wide.region_20.21_spmd.clone, body=%wide.region_19.20_spmd.clone.sunk | while | flops 2162713 | bytes 4721729 | solution.py:93
  429.6 8.0 %collective-permute-start.12 = (f32[8,8192]{1,0:T(8,128)S(1)}, f32[8,8192]{1,0:T(8,128)S(1)}, u32[]{:S(2)}, u32[]{:S(2)}) collective-permute-start(f32[8,8192]{1,0:T(8,128)S(1)} %get-tuple-element.1218), channel_id=1, source_target_pairs={{0,1},{1,2},{2,3},{3,4},{4,5},{5,6},{6,7},{7,8},{8,9},{9,10},{10,1... | collective-permute-start | bytes 786440 | tf_op jit(solution)/shard_map/ppermute | solution.py:21
  441.4 27.8 %while.151 = (s32[]{:T(128)}, f32[8,8192]{1,0:T(8,128)S(1)}, f32[8,16,16]{2,0,1:T(8,128)S(1)}, f32[24,8208]{1,0:T(8,128)S(1)}, s32[]{:T(128)}, /*index=5*/s32[]{...) while((s32[]{:T(128)}, f32[8,8192]{1,0:T(8,128)S(1)}, ...), condition=%wide.region_24.25_spmd.clone, body=%wide.region_23.24_spmd.clone.sunk | while | flops 2162706 | bytes 4721599 | solution.py:71
  470.0 47.3 %all-reduce.18 = (f32[]{:T(128)}, f32[]{:T(128)}) all-reduce(f32[]{:T(128)} %get-tuple-element.1217, f32[]{:T(128)} %fusion.138), channel_id=1, replica_groups=mesh['rows'=8,'scales'=4] {'rows','scales'}, use_global_device_ids=true, to_apply=%region_22.23 | all-reduce | flops 2 | bytes 16 | tf_op jit(solution)/shard_map/psum | solution.py:128
  519.4 18.3 %all-gather.6.cloned.1.call-done = f32[32,8192]{1,0:T(8,128)} async-done(((f32[8,8192]{1,0:T(8,128)}), f32[32,8192]{1,0:T(8,128)}) %all-gather.6.cloned.1.call-update) | async-done | bytes 1048592 | tf_op jit(solution)/shard_map/all_gather | solution.py:134
  548.6 5.5 all-to-all-start.4
  555.2 25.1 %all-to-all-done.4 = f32[32,8,1024]{2,0,1:T(8,128)S(1)} async-done(((f32[32,8,1024]{2,0,1:T(8,128)}), f32[32,8,1024]{2,0,1:T(8,128)S(1)}, u32[]{:S(2)}, u32[]{:S(2)}) %all-to-all-start.4) | async-done | bytes 1048608 | tf_op jit(solution)/shard_map/all_to_all | solution.py:146
  585.4 24.4 %all-to-all-done.3 = f32[32,8,1024]{2,0,1:T(8,128)S(1)} async-done(((f32[32,8,1024]{2,0,1:T(8,128)}), f32[32,8,1024]{2,0,1:T(8,128)S(1)}, u32[]{:S(2)}, u32[]{:S(2)}) %all-to-all-start.3) | async-done | bytes 1048608 | tf_op jit(solution)/shard_map/all_to_all | solution.py:145
  610.2 30.1 %all_to_all.115 = f32[8,32,1024]{2,1,0:T(8,128)S(1)} all-to-all(f32[8,32,1024]{2,1,0:T(8,128)S(1)} %bitcast.71), channel_id=1, replica_groups=mesh['rows'=8,'scales'=4] {'rows'}, dimensions={0} | all-to-all | bytes 2097152 | tf_op jit(solution)/shard_map/all_to_all | solution.py:156
  641.4 24.8 %reduce-scatter.5.cloned.1.call-done = f32[8,8192]{1,0:T(8,128)} async-done(((f32[32,8192]{1,0:T(8,128)}), f32[8,8192]{1,0:T(8,128)}) %reduce-scatter.5.cloned.1.call-update) | async-done | bytes 262160 | tf_op jit(solution)/shard_map/reduce_scatter | solution.py:157
  (391 shorter events, 244.2 us)
Async XLA Ops:
  6.5 219.3 %all-gather.4.cloned.1.call-start = ((), (), s32[]{:S(2)}) async-start(), calls=%async_computation.8 | async-start | bytes 1310720 | tf_op jit(solution)/shard_map/all_gather | solution.py:134
  7.6 50.3 %collective-permute-start.2 = (f32[8,8192]{1,0:T(8,128)S(1)}, f32[8,8192]{1,0:T(8,128)S(1)}, u32[]{:S(2)}, u32[]{:S(2)}) collective-permute-start(f32[8,8192]{1,0:T(8,128)S(1)} %sub.46), channel_id=1, source_target_pairs={{0,1},{1,2},{2,3},{3,4},{4,5},{5,6},{6,7},{7,8},{8,9},{9,10},{10,1... | collective-permute-start | bytes 786440 | tf_op jit(solution)/shard_map/ppermute | solution.py:21
  10.0 47.9 %collective-permute-start.3 = (f32[8,8192]{1,0:T(8,128)S(1)}, f32[8,8192]{1,0:T(8,128)S(1)}, u32[]{:S(2)}, u32[]{:S(2)}) collective-permute-start(f32[8,8192]{1,0:T(8,128)S(1)} %sub.46), channel_id=1, source_target_pairs={{1,0},{2,1},{3,2},{4,3},{5,4},{6,5},{7,6},{8,7},{9,8},{10,9},{11,1... | collective-permute-start | bytes 786440 | tf_op jit(solution)/shard_map/ppermute | solution.py:23
  86.1 10.6 %collective-permute-start.4 = (f32[8,8192]{1,0:T(8,128)S(1)}, f32[8,8192]{1,0:T(8,128)S(1)}, u32[]{:S(2)}, u32[]{:S(2)}) collective-permute-start(f32[8,8192]{1,0:T(8,128)S(1)} %mul.2942), channel_id=1, source_target_pairs={{0,1},{1,2},{2,3},{3,4},{4,5},{5,6},{6,7},{7,8},{8,9},{9,10},{10,1... | collective-permute-start | bytes 786440 | tf_op jit(solution)/shard_map/ppermute | solution.py:21
  88.4 8.4 %collective-permute-start.5 = (f32[8,8192]{1,0:T(8,128)S(1)}, f32[8,8192]{1,0:T(8,128)S(1)}, u32[]{:S(2)}, u32[]{:S(2)}) collective-permute-start(f32[8,8192]{1,0:T(8,128)S(1)} %mul.2942), channel_id=1, source_target_pairs={{1,0},{2,1},{3,2},{4,3},{5,4},{6,5},{7,6},{8,7},{9,8},{10,9},{11,1... | collective-permute-start | bytes 786440 | tf_op jit(solution)/shard_map/ppermute | solution.py:23
  89.7 4.4 collective-permute-start
  92.7 3.8 collective-permute-start.1
  127.3 5.6 collective-permute-start.6
  131.6 3.4 collective-permute-start.7
  135.3 72.4 %copy-start.1 = (f32[8,8192]{1,0:T(8,128)S(1)}, f32[8,8192]{1,0:T(8,128)}, u32[]{:S(2)}) copy-start(f32[8,8192]{1,0:T(8,128)} %param.27) | copy-start | bytes 786436
  236.8 31.7 %all-to-all-start.1 = ((f32[32,8,1024]{2,0,1:T(8,128)}), f32[32,8,1024]{2,0,1:T(8,128)S(1)}, u32[]{:S(2)}, u32[]{:S(2)}) async-start(f32[32,8,1024]{2,0,1:T(8,128)} %bitcast.50), calls=%async_computation.1 | async-start | bytes 2097152 | tf_op jit(solution)/shard_map/all_to_all | solution.py:146
  268.5 29.7 %all-to-all-start = ((f32[32,8,1024]{2,0,1:T(8,128)}), f32[32,8,1024]{2,0,1:T(8,128)S(1)}, u32[]{:S(2)}, u32[]{:S(2)}) async-start(f32[32,8,1024]{2,0,1:T(8,128)} %bitcast.68), calls=%async_computation | async-start | bytes 2097152 | tf_op jit(solution)/shard_map/all_to_all | solution.py:145
  272.3 82.3 %reduce-scatter.3.cloned.1.call-start = ((), (), s32[]{:S(2)}) async-start(), calls=%async_computation.9 | async-start | bytes 1310720 | tf_op jit(solution)/shard_map/reduce_scatter | solution.py:157
  329.8 207.8 %all-gather.6.cloned.1.call-start = ((), (), s32[]{:S(2)}) async-start(), calls=%async_computation.10 | async-start | bytes 1310720 | tf_op jit(solution)/shard_map/all_gather | solution.py:134
  355.6 2.9 collective-permute-start.8
  357.2 3.7 collective-permute-start.9
  389.0 8.2 %collective-permute-start.10 = (f32[8,8192]{1,0:T(8,128)S(1)}, f32[8,8192]{1,0:T(8,128)S(1)}, u32[]{:S(2)}, u32[]{:S(2)}) collective-permute-start(f32[8,8192]{1,0:T(8,128)S(1)} %mul.2961), channel_id=1, source_target_pairs={{0,1},{1,2},{2,3},{3,4},{4,5},{5,6},{6,7},{7,8},{8,9},{9,10},{10,1... | collective-permute-start | bytes 786440 | tf_op jit(solution)/shard_map/ppermute | solution.py:21
  395.7 3.4 collective-permute-start.11
  429.6 9.4 %collective-permute-start.12 = (f32[8,8192]{1,0:T(8,128)S(1)}, f32[8,8192]{1,0:T(8,128)S(1)}, u32[]{:S(2)}, u32[]{:S(2)}) collective-permute-start(f32[8,8192]{1,0:T(8,128)S(1)} %get-tuple-element.1218), channel_id=1, source_target_pairs={{0,1},{1,2},{2,3},{3,4},{4,5},{5,6},{6,7},{7,8},{8,9},{9,10},{10,1... | collective-permute-start | bytes 786440 | tf_op jit(solution)/shard_map/ppermute | solution.py:21
  437.7 3.4 collective-permute-start.13
  441.4 77.2 %copy-start.4 = (f32[8,8192]{1,0:T(8,128)S(1)}, f32[8,8192]{1,0:T(8,128)}, u32[]{:S(2)}) copy-start(f32[8,8192]{1,0:T(8,128)} %reduce-scatter.3.cloned.1.call-done) | copy-start | bytes 786436
  548.6 31.7 %all-to-all-start.4 = ((f32[32,8,1024]{2,0,1:T(8,128)}), f32[32,8,1024]{2,0,1:T(8,128)S(1)}, u32[]{:S(2)}, u32[]{:S(2)}) async-start(f32[32,8,1024]{2,0,1:T(8,128)} %bitcast.48), calls=%async_computation.5 | async-start | bytes 2097152 | tf_op jit(solution)/shard_map/all_to_all | solution.py:146
  580.3 29.6 %all-to-all-start.3 = ((f32[32,8,1024]{2,0,1:T(8,128)}), f32[32,8,1024]{2,0,1:T(8,128)S(1)}, u32[]{:S(2)}, u32[]{:S(2)}) async-start(f32[32,8,1024]{2,0,1:T(8,128)} %bitcast.49), calls=%async_computation.4 | async-start | bytes 2097152 | tf_op jit(solution)/shard_map/all_to_all | solution.py:145
  583.9 82.3 %reduce-scatter.5.cloned.1.call-start = ((), (), s32[]{:S(2)}) async-start(), calls=%async_computation.11 | async-start | bytes 1310720 | tf_op jit(solution)/shard_map/reduce_scatter | solution.py:157
  (5 other events, 63.7 us)
Sparse Core Ops, SparseCore 0:
  208.6 17.2 all-gather.3
  329.9 24.6 reduce-scatter.2
  519.5 18.0 all-gather.5
  641.5 24.6 reduce-scatter.4
where the time goes:
time: 674 us; the launch traced here: 673 us
  blocking collectives  196 us (29%)
  waiting for transfers between devices  195 us (29%)
  other arithmetic  156 us (23%)
  starting transfers between devices  56.1 us (8%)
  local copies, waits for them, and re-layouts  49.5 us (7%)
  between operations  17.6 us (3%)
    psum x2, blocking collectives, body(): lax.psum((jnp.sum(descent * descent), jnp.sum(hessian_weight * blurred *...  89.8 us
    add x64, other arithmetic, forward_add_tap_row(): summed + tap_weights[:, column:column + 1] * shifted[:, column:column + c...  81 us
    all_to_all x2, blocking collectives, body(): lax.all_to_all(kept, 'rows', split_axis=0, concat_axis=1, tiled=True)  60.3 us
    all_to_all x2, waiting for transfers between devices, body(): lax.all_to_all(upper, 'rows', split_axis=1, concat_axis=0, tiled=True)  50.2 us
    reduce_scatter x2, waiting for transfers between devices, body(): lax.psum_scatter(contribution, 'scales', scatter_dimension=0, tiled=True)  49.5 us
    all_to_all x2, waiting for transfers between devices, body(): lax.all_to_all(lower, 'rows', split_axis=1, concat_axis=0, tiled=True)  48.3 us
    all_gather x1, blocking collectives, body(): tiles_in = lax.all_gather(psf_tiles, ('rows', 'scales'), axis=0, tiled=True)  45.4 us
    add x32, other arithmetic, adjoint_add_tap_row(): summed + tap_weights[:, column:column + 1] * shifted[:, offset_col:offset...  43.6 us
  transfers between devices with their start and end apart: 22, of which 13 were waited for; matrix products, arithmetic and copies ran while one was open for 1% of the time, Pallas kernels for 0%

commit v1 on v0

--- a/solution.py
+++ b/solution.py
@@ -131,7 +131,27 @@
         )
         step_size = totals[0] / totals[1]
         trial = current - step_size * descent
-        stripe = lax.all_gather(trial, "scales", axis=0, tiled=True)
+        w_next, far_arr, block_out = (
+            lax.axis_size("scales"),
+            lax.axis_index("scales"),
+            trial.shape[0],
+        )
+        gallery = tuple(((i0, (i0 + 1) % w_next) for i0 in range(w_next)))
+        stripe = jnp.zeros((*trial.shape[:0], w_next * block_out, *trial.shape[1:]), trial.dtype)
+        stripe = lax.dynamic_update_slice_in_dim(stripe, trial, far_arr * block_out, axis=0)
+        series = tuple(((i0, (i0 - 1) % w_next) for i0 in range(w_next)))
+        met_up = w_next // 2
+        y2 = before = trial
+        for q in range(1, met_up + 1):
+            y2 = lax.ppermute(y2, "scales", gallery)
+            stripe = lax.dynamic_update_slice_in_dim(
+                stripe, y2, (far_arr - q) % w_next * block_out, axis=0
+            )
+            if q < w_next - met_up:
+                before = lax.ppermute(before, "scales", series)
+                stripe = lax.dynamic_update_slice_in_dim(
+                    stripe, before, (far_arr + q) % w_next * block_out, axis=0
+                )
         smooth = stripe
         lower = jnp.zeros_like(stripe)
         upper = jnp.zeros_like(stripe)

time: 674 us -> 654 us (0.970)
  waiting for transfers between devices: 195 us -> 172 us
  starting transfers between devices: 56.1 us -> 65.8 us
  other arithmetic: 156 us -> 148 us
    all_gather x2 -> x0, waiting for transfers between devices: 35.6 us -> none  [body(): stripe = lax.all_gather(trial, 'scales', axis=0, tiled=True)]
    ppermute x0 -> x6, waiting for transfers between devices: none -> 14.1 us  [the longest x4 14.1 us: body(): y2 = lax.ppermute(y2, 'scales', gallery)]
    ppermute x0 -> x6, starting transfers between devices: none -> 9.03 us  [the longest x4 5.64 us: body(): y2 = lax.ppermute(y2, 'scales', gallery)]
  transfers between devices with their start and end apart: 22 -> 26, of which waited for: 13 -> 15; matrix products, arithmetic and copies ran while one was open for 1% -> 1% of each run, Pallas kernels for 0% -> 0%
where the time goes in v1:
time: 654 us; the launch traced here: 652 us
  blocking collectives  195 us (30%)
  waiting for transfers between devices  172 us (26%)
  other arithmetic  148 us (23%)
  starting transfers between devices  65.8 us (10%)
  local copies, waits for them, and re-layouts  49.7 us (8%)
  between operations  18 us (3%)
    psum x2, blocking collectives, body(): lax.psum((jnp.sum(descent * descent), jnp.sum(hessian_weight * blurred *...  89.6 us
    add x64, other arithmetic, forward_add_tap_row(): summed + tap_weights[:, column:column + 1] * shifted[:, column:column + c...  81 us
    all_to_all x2, blocking collectives, body(): lax.all_to_all(kept, 'rows', split_axis=0, concat_axis=1, tiled=True)  60.3 us
    all_to_all x2, waiting for transfers between devices, body(): lax.all_to_all(upper, 'rows', split_axis=1, concat_axis=0, tiled=True)  51.6 us
    all_to_all x2, waiting for transfers between devices, body(): lax.all_to_all(lower, 'rows', split_axis=1, concat_axis=0, tiled=True)  48.8 us
    reduce_scatter x2, waiting for transfers between devices, body(): lax.psum_scatter(contribution, 'scales', scatter_dimension=0, tiled=True)  46.2 us
    all_gather x1, blocking collectives, body(): tiles_in = lax.all_gather(psf_tiles, ('rows', 'scales'), axis=0, tiled=True)  45.4 us
    add x32, other arithmetic, adjoint_add_tap_row(): summed + tap_weights[:, column:column + 1] * shifted[:, offset_col:offset...  43.6 us
  transfers between devices with their start and end apart: 26, of which 15 were waited for; matrix products, arithmetic and copies ran while one was open for 1% of the time, Pallas kernels for 0%

profile of v1, /device:TPU:0, one launch (start us, length us, event | category | flops | bytes accessed | tf_op | source)
XLA Modules:
  0.0 652.4 jit_solution(17945894191161241159)
XLA Ops:
  12.2 45.4 %all-gather = f32[32,1,256]{2,1,0:T(1,128)S(1)} all-gather(f32[1,1,256]{2,1,0:T(1,128)} %bitcast.79), channel_id=1, replica_groups=mesh['rows'=8,'scales'=4] {'rows','scales'}, dimensions={0}, use_global_device_ids=true | all-gather | bytes 33792 | tf_op jit(solution)/shard_map/all_gather | solution.py:105
  58.2 27.8 %while.146 = (s32[]{:T(128)}, f32[8,8192]{1,0:T(8,128)S(1)}, f32[8,16,16]{2,0,1:T(8,128)S(1)}, f32[24,8208]{1,0:T(8,128)S(1)}, s32[]{:T(128)}, /*index=5*/s32[]{...) while((s32[]{:T(128)}, f32[8,8192]{1,0:T(8,128)S(1)}, ...), condition=%wide.region_2.3_spmd.clone, body=%wide.region_1.2_spmd.clone.sunk | while | flops 2162706 | bytes 4721599 | solution.py:71
  97.0 29.6 %while.147 = (s32[]{:T(128)}, f32[8,8192]{1,0:T(8,128)S(1)}, f32[24,16,16]{2,0,1:T(8,128)S(1)}, f32[24,8208]{1,0:T(8,128)S(1)}, s32[]{:T(128)}, /*index=5*/s32[]...) while((s32[]{:T(128)}, f32[8,8192]{1,0:T(8,128)S(1)}, ...), condition=%wide.region_4.5_spmd.clone, body=%wide.region_3.4_spmd.clone.sunk | while | flops 2162713 | bytes 4721729 | solution.py:93
  127.3 4.3 collective-permute-start.6
  135.3 27.8 %while.148 = (s32[]{:T(128)}, f32[8,8192]{1,0:T(8,128)S(1)}, f32[8,16,16]{2,0,1:T(8,128)S(1)}, f32[24,8208]{1,0:T(8,128)S(1)}, s32[]{:T(128)}, /*index=5*/s32[]{...) while((s32[]{:T(128)}, f32[8,8192]{1,0:T(8,128)S(1)}, ...), condition=%wide.region_8.9_spmd.clone, body=%wide.region_7.8_spmd.clone.sunk | while | flops 2162706 | bytes 4721599 | solution.py:71
  163.8 42.3 %all-reduce.19 = (f32[]{:T(128)}, f32[]{:T(128)}) all-reduce(f32[]{:T(128)} %get-tuple-element.1249, f32[]{:T(128)} %fusion.137), channel_id=1, replica_groups=mesh['rows'=8,'scales'=4] {'rows','scales'}, use_global_device_ids=true, to_apply=%region_6.7 | all-reduce | flops 2 | bytes 16 | tf_op jit(solution)/shard_map/psum | solution.py:128
  209.4 4.1 collective-permute-done.8
  227.2 5.6 all-to-all-start.1
  233.9 25.9 %all-to-all-done.1 = f32[32,8,1024]{2,0,1:T(8,128)S(1)} async-done(((f32[32,8,1024]{2,0,1:T(8,128)}), f32[32,8,1024]{2,0,1:T(8,128)S(1)}, u32[]{:S(2)}, u32[]{:S(2)}) %all-to-all-start.1) | async-done | bytes 1048608 | tf_op jit(solution)/shard_map/all_to_all | solution.py:166
  265.7 23.9 %all-to-all-done = f32[32,8,1024]{2,0,1:T(8,128)S(1)} async-done(((f32[32,8,1024]{2,0,1:T(8,128)}), f32[32,8,1024]{2,0,1:T(8,128)S(1)}, u32[]{:S(2)}, u32[]{:S(2)}) %all-to-all-start) | async-done | bytes 1048608 | tf_op jit(solution)/shard_map/all_to_all | solution.py:165
  289.9 30.1 %all_to_all.114 = f32[8,32,1024]{2,1,0:T(8,128)S(1)} all-to-all(f32[8,32,1024]{2,1,0:T(8,128)S(1)} %bitcast.72), channel_id=1, replica_groups=mesh['rows'=8,'scales'=4] {'rows'}, dimensions={0} | all-to-all | bytes 2097152 | tf_op jit(solution)/shard_map/all_to_all | solution.py:176
  321.2 23.1 %reduce-scatter.3.cloned.1.call-done = f32[8,8192]{1,0:T(8,128)} async-done(((f32[32,8192]{1,0:T(8,128)}), f32[8,8192]{1,0:T(8,128)}) %reduce-scatter.3.cloned.1.call-update) | async-done | bytes 262160 | tf_op jit(solution)/shard_map/reduce_scatter | solution.py:177
  350.8 27.8 %while.149 = (s32[]{:T(128)}, f32[8,8192]{1,0:T(8,128)S(1)}, f32[8,16,16]{2,0,1:T(8,128)S(1)}, f32[24,8208]{1,0:T(8,128)S(1)}, s32[]{:T(128)}, /*index=5*/s32[]{...) while((s32[]{:T(128)}, f32[8,8192]{1,0:T(8,128)S(1)}, ...), condition=%wide.region_18.19_spmd.clone, body=%wide.region_17.18_spmd.clone.sunk | while | flops 2162706 | bytes 4721599 | solution.py:71
  378.7 6.7 %collective-permute-start.13 = (f32[8,8192]{1,0:T(8,128)S(1)}, f32[8,8192]{1,0:T(8,128)S(1)}, u32[]{:S(2)}, u32[]{:S(2)}) collective-permute-start(f32[8,8192]{1,0:T(8,128)S(1)} %mul.2981), channel_id=1, source_target_pairs={{0,1},{1,2},{2,3},{3,4},{4,5},{5,6},{6,7},{7,8},{8,9},{9,10},{10,1... | collective-permute-start | bytes 786440 | tf_op jit(solution)/shard_map/ppermute | solution.py:21
  389.1 29.6 %while.150 = (s32[]{:T(128)}, f32[8,8192]{1,0:T(8,128)S(1)}, f32[24,16,16]{2,0,1:T(8,128)S(1)}, f32[24,8208]{1,0:T(8,128)S(1)}, s32[]{:T(128)}, /*index=5*/s32[]...) while((s32[]{:T(128)}, f32[8,8192]{1,0:T(8,128)S(1)}, ...), condition=%wide.region_20.21_spmd.clone, body=%wide.region_19.20_spmd.clone.sunk | while | flops 2162713 | bytes 4721729 | solution.py:93
  419.4 8.0 %collective-permute-start.15 = (f32[8,8192]{1,0:T(8,128)S(1)}, f32[8,8192]{1,0:T(8,128)S(1)}, u32[]{:S(2)}, u32[]{:S(2)}) collective-permute-start(f32[8,8192]{1,0:T(8,128)S(1)} %get-tuple-element.1244), channel_id=1, source_target_pairs={{0,1},{1,2},{2,3},{3,4},{4,5},{5,6},{6,7},{7,8},{8,9},{9,10},{10,1... | collective-permute-start | bytes 786440 | tf_op jit(solution)/shard_map/ppermute | solution.py:21
  431.1 27.8 %while.151 = (s32[]{:T(128)}, f32[8,8192]{1,0:T(8,128)S(1)}, f32[8,16,16]{2,0,1:T(8,128)S(1)}, f32[24,8208]{1,0:T(8,128)S(1)}, s32[]{:T(128)}, /*index=5*/s32[]{...) while((s32[]{:T(128)}, f32[8,8192]{1,0:T(8,128)S(1)}, ...), condition=%wide.region_24.25_spmd.clone, body=%wide.region_23.24_spmd.clone.sunk | while | flops 2162706 | bytes 4721599 | solution.py:71
  459.7 47.4 %all-reduce.18 = (f32[]{:T(128)}, f32[]{:T(128)}) all-reduce(f32[]{:T(128)} %get-tuple-element.1243, f32[]{:T(128)} %fusion.138), channel_id=1, replica_groups=mesh['rows'=8,'scales'=4] {'rows','scales'}, use_global_device_ids=true, to_apply=%region_22.23 | all-reduce | flops 2 | bytes 16 | tf_op jit(solution)/shard_map/psum | solution.py:128
  510.3 4.1 collective-permute-done.17
  528.0 5.8 all-to-all-start.4
  534.9 25.7 %all-to-all-done.4 = f32[32,8,1024]{2,0,1:T(8,128)S(1)} async-done(((f32[32,8,1024]{2,0,1:T(8,128)}), f32[32,8,1024]{2,0,1:T(8,128)S(1)}, u32[]{:S(2)}, u32[]{:S(2)}) %all-to-all-start.4) | async-done | bytes 1048608 | tf_op jit(solution)/shard_map/all_to_all | solution.py:166
  566.0 24.9 %all-to-all-done.3 = f32[32,8,1024]{2,0,1:T(8,128)S(1)} async-done(((f32[32,8,1024]{2,0,1:T(8,128)}), f32[32,8,1024]{2,0,1:T(8,128)S(1)}, u32[]{:S(2)}, u32[]{:S(2)}) %all-to-all-start.3) | async-done | bytes 1048608 | tf_op jit(solution)/shard_map/all_to_all | solution.py:165
  591.2 30.1 %all_to_all.115 = f32[8,32,1024]{2,1,0:T(8,128)S(1)} all-to-all(f32[8,32,1024]{2,1,0:T(8,128)S(1)} %bitcast.71), channel_id=1, replica_groups=mesh['rows'=8,'scales'=4] {'rows'}, dimensions={0} | all-to-all | bytes 2097152 | tf_op jit(solution)/shard_map/all_to_all | solution.py:176
  622.5 23.1 %reduce-scatter.5.cloned.1.call-done = f32[8,8192]{1,0:T(8,128)} async-done(((f32[32,8192]{1,0:T(8,128)}), f32[8,8192]{1,0:T(8,128)}) %reduce-scatter.5.cloned.1.call-update) | async-done | bytes 262160 | tf_op jit(solution)/shard_map/reduce_scatter | solution.py:177
  (401 shorter events, 252.1 us)
Async XLA Ops:
  7.6 50.3 %collective-permute-start.2 = (f32[8,8192]{1,0:T(8,128)S(1)}, f32[8,8192]{1,0:T(8,128)S(1)}, u32[]{:S(2)}, u32[]{:S(2)}) collective-permute-start(f32[8,8192]{1,0:T(8,128)S(1)} %sub.54), channel_id=1, source_target_pairs={{0,1},{1,2},{2,3},{3,4},{4,5},{5,6},{6,7},{7,8},{8,9},{9,10},{10,1... | collective-permute-start | bytes 786440 | tf_op jit(solution)/shard_map/ppermute | solution.py:21
  10.0 47.9 %collective-permute-start.3 = (f32[8,8192]{1,0:T(8,128)S(1)}, f32[8,8192]{1,0:T(8,128)S(1)}, u32[]{:S(2)}, u32[]{:S(2)}) collective-permute-start(f32[8,8192]{1,0:T(8,128)S(1)} %sub.54), channel_id=1, source_target_pairs={{1,0},{2,1},{3,2},{4,3},{5,4},{6,5},{7,6},{8,7},{9,8},{10,9},{11,1... | collective-permute-start | bytes 786440 | tf_op jit(solution)/shard_map/ppermute | solution.py:23
  86.1 10.6 %collective-permute-start.4 = (f32[8,8192]{1,0:T(8,128)S(1)}, f32[8,8192]{1,0:T(8,128)S(1)}, u32[]{:S(2)}, u32[]{:S(2)}) collective-permute-start(f32[8,8192]{1,0:T(8,128)S(1)} %mul.2958), channel_id=1, source_target_pairs={{0,1},{1,2},{2,3},{3,4},{4,5},{5,6},{6,7},{7,8},{8,9},{9,10},{10,1... | collective-permute-start | bytes 786440 | tf_op jit(solution)/shard_map/ppermute | solution.py:21
  88.4 8.4 %collective-permute-start.5 = (f32[8,8192]{1,0:T(8,128)S(1)}, f32[8,8192]{1,0:T(8,128)S(1)}, u32[]{:S(2)}, u32[]{:S(2)}) collective-permute-start(f32[8,8192]{1,0:T(8,128)S(1)} %mul.2958), channel_id=1, source_target_pairs={{1,0},{2,1},{3,2},{4,3},{5,4},{6,5},{7,6},{8,7},{9,8},{10,9},{11,1... | collective-permute-start | bytes 786440 | tf_op jit(solution)/shard_map/ppermute | solution.py:23
  89.7 4.4 collective-permute-start
  92.7 3.8 collective-permute-start.1
  127.3 5.6 collective-permute-start.6
  131.6 3.4 collective-permute-start.7
  207.6 5.8 collective-permute-start.8
  207.8 8.5 %collective-permute-start.9 = (f32[8,8192]{1,0:T(8,128)S(1)}, f32[8,8192]{1,0:T(8,128)S(1)}, u32[]{:S(2)}, u32[]{:S(2)}) collective-permute-start(f32[8,8192]{1,0:T(8,128)S(1)} %get-tuple-element.1248), channel_id=1, source_target_pairs={{0,3},{1,0},{2,1},{3,2},{4,7},{5,4},{6,5},{7,6},{8,11},{9,8},{10,9... | collective-permute-start | bytes 786440 | tf_op jit(solution)/shard_map/ppermute | solution.py:151
  213.5 5.8 collective-permute-start.10
  227.2 32.6 %all-to-all-start.1 = ((f32[32,8,1024]{2,0,1:T(8,128)}), f32[32,8,1024]{2,0,1:T(8,128)S(1)}, u32[]{:S(2)}, u32[]{:S(2)}) async-start(f32[32,8,1024]{2,0,1:T(8,128)} %bitcast.50), calls=%async_computation.1 | async-start | bytes 2097152 | tf_op jit(solution)/shard_map/all_to_all | solution.py:166
  259.8 29.8 %all-to-all-start = ((f32[32,8,1024]{2,0,1:T(8,128)}), f32[32,8,1024]{2,0,1:T(8,128)S(1)}, u32[]{:S(2)}, u32[]{:S(2)}) async-start(f32[32,8,1024]{2,0,1:T(8,128)} %bitcast.68), calls=%async_computation | async-start | bytes 2097152 | tf_op jit(solution)/shard_map/all_to_all | solution.py:165
  263.6 80.7 %reduce-scatter.3.cloned.1.call-start = ((), (), s32[]{:S(2)}) async-start(), calls=%async_computation.8 | async-start | bytes 1310720 | tf_op jit(solution)/shard_map/reduce_scatter | solution.py:177
  346.9 3.7 collective-permute-start.12
  378.7 8.2 %collective-permute-start.13 = (f32[8,8192]{1,0:T(8,128)S(1)}, f32[8,8192]{1,0:T(8,128)S(1)}, u32[]{:S(2)}, u32[]{:S(2)}) collective-permute-start(f32[8,8192]{1,0:T(8,128)S(1)} %mul.2981), channel_id=1, source_target_pairs={{0,1},{1,2},{2,3},{3,4},{4,5},{5,6},{6,7},{7,8},{8,9},{9,10},{10,1... | collective-permute-start | bytes 786440 | tf_op jit(solution)/shard_map/ppermute | solution.py:21
  385.4 3.4 collective-permute-start.14
  419.4 9.3 %collective-permute-start.15 = (f32[8,8192]{1,0:T(8,128)S(1)}, f32[8,8192]{1,0:T(8,128)S(1)}, u32[]{:S(2)}, u32[]{:S(2)}) collective-permute-start(f32[8,8192]{1,0:T(8,128)S(1)} %get-tuple-element.1244), channel_id=1, source_target_pairs={{0,1},{1,2},{2,3},{3,4},{4,5},{5,6},{6,7},{7,8},{8,9},{9,10},{10,1... | collective-permute-start | bytes 786440 | tf_op jit(solution)/shard_map/ppermute | solution.py:21
  508.5 5.9 collective-permute-start.17
  508.5 8.6 %collective-permute-start.18 = (f32[8,8192]{1,0:T(8,128)S(1)}, f32[8,8192]{1,0:T(8,128)S(1)}, u32[]{:S(2)}, u32[]{:S(2)}) collective-permute-start(f32[8,8192]{1,0:T(8,128)S(1)} %get-tuple-element.1242), channel_id=1, source_target_pairs={{0,3},{1,0},{2,1},{3,2},{4,7},{5,4},{6,5},{7,6},{8,11},{9,8},{10,9... | collective-permute-start | bytes 786440 | tf_op jit(solution)/shard_map/ppermute | solution.py:151
  514.3 5.8 collective-permute-start.19
  528.0 32.6 %all-to-all-start.4 = ((f32[32,8,1024]{2,0,1:T(8,128)}), f32[32,8,1024]{2,0,1:T(8,128)S(1)}, u32[]{:S(2)}, u32[]{:S(2)}) async-start(f32[32,8,1024]{2,0,1:T(8,128)} %bitcast.48), calls=%async_computation.5 | async-start | bytes 2097152 | tf_op jit(solution)/shard_map/all_to_all | solution.py:166
  560.6 30.3 %all-to-all-start.3 = ((f32[32,8,1024]{2,0,1:T(8,128)}), f32[32,8,1024]{2,0,1:T(8,128)S(1)}, u32[]{:S(2)}, u32[]{:S(2)}) async-start(f32[32,8,1024]{2,0,1:T(8,128)} %bitcast.49), calls=%async_computation.4 | async-start | bytes 2097152 | tf_op jit(solution)/shard_map/all_to_all | solution.py:165
  564.5 81.1 %reduce-scatter.5.cloned.1.call-start = ((), (), s32[]{:S(2)}) async-start(), calls=%async_computation.9 | async-start | bytes 1310720 | tf_op jit(solution)/shard_map/reduce_scatter | solution.py:177
  (7 other events, 161.5 us)
Sparse Core Ops, SparseCore 0:
  321.3 22.9 reduce-scatter.2
  622.6 22.9 reduce-scatter.4
